TPU v7x, 32 devices: a whole 2x2x4 slice. The times are simulated.
32 devices in a mesh: dev: 32 (over z, y, x, core).
Axes of the slice: x: 2, y: 2, z: 4, core: 2. Of those that a mesh axis runs over, the one named last changes fastest.
Arguments:
- images: bfloat16 [256, 768, 1536], P('dev'), may hold values from -6 to 6
- legendre: bfloat16 [32, 704, 768], P('dev'), may hold values from -0.21875 to 0.21875
- leakage: float32 [32, 3, 13, 704], P('dev'), may hold values from -1 to 1
Outputs:
- modes: float32 [32, 704, 512], P('dev')
All inputs are finite; a program needn't handle non-finite values.
Results may differ from a plain program's by a relative error of at most 0.0053.
Values may be sent and summed in bfloat16 or wider, within the bound.
A program may use at most 128 MiB of HBM per device.

v0:
```python
import math

import jax
import jax.numpy as jnp
from jax import lax
from jax.sharding import PartitionSpec as P

BLK = 64
BAND = 6


def padded_2(cells, sides, width):
    for axis, dim in sides:
        count = lax.axis_size(axis)
        ends = count - 1
        head = lax.slice_in_dim(cells, 0, width, axis=dim)
        tail = lax.slice_in_dim(cells, cells.shape[dim] - width, cells.shape[dim], axis=dim)
        cells = jnp.concatenate(
            [
                lax.ppermute(tail, axis, [(i, (i + 1) % count) for i in range(ends)]),
                cells,
                lax.ppermute(head, axis, [((i + 1) % count, i) for i in range(ends)]),
            ],
            axis=dim,
        )
    return cells


def lon_table(nlon, norders):
    index = jnp.arange(nlon, dtype=jnp.int32)[None, :]
    order = jnp.arange(norders, dtype=jnp.int32)[:, None]
    phase = (index * order % nlon).astype(jnp.float32)
    angle = 2.0 * math.pi * phase / nlon
    table = jnp.stack([jnp.cos(angle), -jnp.sin(angle)], axis=1) / math.sqrt(nlon)
    return table.reshape(2 * norders, nlon).astype(jnp.bfloat16)


def time_table(ntimes):
    index = jnp.arange(ntimes, dtype=jnp.int32)
    phase = (index[:, None] * index[None, :] % ntimes).astype(jnp.float32)
    angle = 2.0 * math.pi * phase / ntimes
    cosine = jnp.cos(angle)
    sine = jnp.sin(angle)
    upper = jnp.concatenate([cosine, -sine], axis=1)
    lower = jnp.concatenate([sine, cosine], axis=1)
    return (jnp.concatenate([upper, lower], axis=0) / math.sqrt(ntimes)).astype(jnp.bfloat16)


def transform_images(table, block):
    out = jnp.einsum("kn,tan->kta", table, block, preferred_element_type=jnp.float32)
    return out.astype(jnp.bfloat16)


def on_device(images, legendre, leakage):
    devices = lax.axis_size("dev")
    here = lax.axis_index("dev")
    t_local, nlat, nlon = images.shape
    m_local, degrees_all, _ = legendre.shape
    norders = m_local * devices
    ntimes = t_local * devices
    table = lon_table(nlon, norders)
    whole = transform_images(table, images).reshape(norders, 2, t_local, nlat)
    gathered = lax.all_to_all(whole, "dev", split_axis=0, concat_axis=2, tiled=True)
    wtable = time_table(ntimes)
    nblocks = degrees_all // BLK
    local = 0
    order = here * m_local + local
    flat = gathered[local].reshape(2 * ntimes, nlat)
    rows_table = legendre[local]

    def one_block(block, spectra, order=order, flat=flat, rows_table=rows_table):
        start = block * BLK
        rows = lax.dynamic_slice_in_dim(rows_table, start, BLK, 0)
        coef = lax.dot_general(
            rows, flat, (((1,), (1,)), ((), ())), preferred_element_type=jnp.float32
        )
        degree = start + jnp.arange(BLK, dtype=jnp.int32)
        coef = jnp.where((degree >= order)[:, None], coef, jnp.float32(0.0)).astype(jnp.bfloat16)
        result = jnp.dot(coef, wtable, preferred_element_type=jnp.float32)
        return lax.dynamic_update_slice_in_dim(spectra, result, start, 0)

    first = order // BLK
    empty = jnp.zeros((degrees_all, 2 * ntimes), jnp.float32)
    spectra_list = [lax.fori_loop(first, jnp.int32(nblocks), one_block, empty)]
    spectra = jnp.stack(spectra_list, axis=0)
    padded = padded_2(spectra, (("dev", 0),), 1)
    padded = jnp.pad(padded, ((0, 0), (BAND, BAND), (0, 0)))
    degrees = jnp.arange(degrees_all, dtype=jnp.int32)
    local = 0
    order = here * m_local + local
    coeffs = leakage[local]
    total = jnp.zeros((degrees_all, 2 * ntimes), jnp.float32)
    for shift in range(3):
        for offset in range(2 * BAND + 1):
            total = (
                total
                + coeffs[shift, offset][:, None]
                * padded[local + shift, offset : offset + degrees_all]
            )
    outputs = [jnp.where((degrees >= order)[:, None], total, jnp.float32(0.0))]
    return jnp.stack(outputs, axis=0)


def solution(mesh):
    placed = (P("dev", None, None), P("dev", None, None), P("dev", None, None, None))
    return jax.shard_map(
        on_device, mesh=mesh, in_specs=placed, out_specs=P("dev", None, None), check_vma=False
    )
```

profile of v0, /device:TPU:1, one launch (start us, length us, event | category | flops | bytes accessed | tf_op | source)
XLA Modules:
  0.0 104.0 jit_solution(8679333870553698052)
XLA Ops:
  0.0 0.8 sine_negate_fusion
  0.9 0.2 copy.10
  1.1 0.1 reshape.393
  1.2 12.1 %convolution_convert_fusion = bf16[64,8,768]{2,0,1:T(8,128)(2,1)S(1)} fusion(bf16[64,1536,1]{1,0,2:T(8,128)(2,1)S(1)} %reshape.393, bf16[8,768,1536]{2,1,0:T(8,128)(2,1)} %param.5), kind=kOutput, calls=%fused_computation.89 | convolution fusion | flops 1208352768 | bytes 19857408 | tf_op jit(solution)/shard_map/kn,tan->kta/dot_general | solution.py:50
  13.3 0.3 reshape.392
  13.6 1.4 %copy.11 = bf16[32,2,8,768]{3,1,2,0:T(2,128)(2,1)} copy(bf16[32,2,8,768]{3,1,0,2:T(2,128)(2,1)S(1)} %reshape.392) | data formatting | bytes 1572864 | tf_op jit(solution)/shard_map/reshape | solution.py:62
  15.0 7.1 %all-to-all-start = ((bf16[32,2,8,768]{3,1,2,0:T(2,128)(2,1)}), bf16[32,2,8,768]{3,1,2,0:T(2,128)(2,1)S(1)}, u32[]{:S(2)}, u32[]{:S(2)}) async-start(bf16[32,2,8,768]{3,1,2,0:T(2,128)(2,1)} %copy.11), calls=%async_computation | async-start | bytes 1572864 | tf_op jit(solution)/shard_map/all_to_all | solution.py:63
  22.1 1.0 fusion.64
  23.1 1.0 fusion.62
  24.1 0.1 fusion.48
  24.2 18.1 %all-to-all-done = bf16[32,2,8,768]{3,1,2,0:T(2,128)(2,1)S(1)} async-done(((bf16[32,2,8,768]{3,1,2,0:T(2,128)(2,1)}), bf16[32,2,8,768]{3,1,2,0:T(2,128)(2,1)S(1)}, u32[]{:S(2)}, u32[]{:S(2)}) %all-to-all-start) | async-done | bytes 786464 | tf_op jit(solution)/shard_map/all_to_all | solution.py:63
  42.3 0.1 copy.12
  42.4 0.2 broadcast_in_dim.34
  42.6 0.0 copy-start
  42.6 16.0 %while.10 = (s32[]{:T(128)}, f32[704,512]{1,0:T(8,128)S(1)}, s32[]{:T(128)}, bf16[704,768]{1,0:T(8,128)(2,1)}, bf16[512,768]{1,0:T(8,128)(2,1)S(1)}, /*index=5*/...) while((s32[]{:T(128)}, f32[704,512]{1,0:T(8,128)S(1)}, s32[]{:T(128)}, ...), condition=%wide.region_1.2_spmd, body=%wide.region_0.1_spmd.sunk | while | flops 83951752 | bytes 1541851 | solution.py:84
  42.6 1.4 %convolution_dynamic-update-slice_fusion.2 = f32[704,512]{1,0:T(8,128)S(1)} fusion(f32[704,512]{1,0:T(8,128)S(1)} %get-tuple-element.140, s32[]{:T(128)S(6)} %select_n.82, bf16[512,512]{1,0:T(8,128)(2,1)S(1)} %get-tuple-element.154, bf16[512,768]{1,0:T(8,128)(2,1)S(1)} %get-tuple-element.153, bf16[704,768]{1,0:T(8,128)(2,1)} %get-tuple-element.152, ...), kind=kOutput, calls=%fused_computation.clone.1 | convolution fusion | flops 83951616 | bytes 1541632 | tf_op jit(solution)/shard_map/while/body/dot_general | solution.py:79
  44.1 1.4 %convolution_dynamic-update-slice_fusion.2 = f32[704,512]{1,0:T(8,128)S(1)} fusion(f32[704,512]{1,0:T(8,128)S(1)} %get-tuple-element.140, s32[]{:T(128)S(6)} %select_n.82, bf16[512,512]{1,0:T(8,128)(2,1)S(1)} %get-tuple-element.154, bf16[512,768]{1,0:T(8,128)(2,1)S(1)} %get-tuple-element.153, bf16[704,768]{1,0:T(8,128)(2,1)} %get-tuple-element.152, ...), kind=kOutput, calls=%fused_computation.clone.1 | convolution fusion | flops 83951616 | bytes 1541632 | tf_op jit(solution)/shard_map/while/body/dot_general | solution.py:79
  45.5 1.4 %convolution_dynamic-update-slice_fusion.2 = f32[704,512]{1,0:T(8,128)S(1)} fusion(f32[704,512]{1,0:T(8,128)S(1)} %get-tuple-element.140, s32[]{:T(128)S(6)} %select_n.82, bf16[512,512]{1,0:T(8,128)(2,1)S(1)} %get-tuple-element.154, bf16[512,768]{1,0:T(8,128)(2,1)S(1)} %get-tuple-element.153, bf16[704,768]{1,0:T(8,128)(2,1)} %get-tuple-element.152, ...), kind=kOutput, calls=%fused_computation.clone.1 | convolution fusion | flops 83951616 | bytes 1541632 | tf_op jit(solution)/shard_map/while/body/dot_general | solution.py:79
  47.0 1.4 %convolution_dynamic-update-slice_fusion.2 = f32[704,512]{1,0:T(8,128)S(1)} fusion(f32[704,512]{1,0:T(8,128)S(1)} %get-tuple-element.140, s32[]{:T(128)S(6)} %select_n.82, bf16[512,512]{1,0:T(8,128)(2,1)S(1)} %get-tuple-element.154, bf16[512,768]{1,0:T(8,128)(2,1)S(1)} %get-tuple-element.153, bf16[704,768]{1,0:T(8,128)(2,1)} %get-tuple-element.152, ...), kind=kOutput, calls=%fused_computation.clone.1 | convolution fusion | flops 83951616 | bytes 1541632 | tf_op jit(solution)/shard_map/while/body/dot_general | solution.py:79
  48.4 1.4 %convolution_dynamic-update-slice_fusion.2 = f32[704,512]{1,0:T(8,128)S(1)} fusion(f32[704,512]{1,0:T(8,128)S(1)} %get-tuple-element.140, s32[]{:T(128)S(6)} %select_n.82, bf16[512,512]{1,0:T(8,128)(2,1)S(1)} %get-tuple-element.154, bf16[512,768]{1,0:T(8,128)(2,1)S(1)} %get-tuple-element.153, bf16[704,768]{1,0:T(8,128)(2,1)} %get-tuple-element.152, ...), kind=kOutput, calls=%fused_computation.clone.1 | convolution fusion | flops 83951616 | bytes 1541632 | tf_op jit(solution)/shard_map/while/body/dot_general | solution.py:79
  49.9 1.4 %convolution_dynamic-update-slice_fusion.2 = f32[704,512]{1,0:T(8,128)S(1)} fusion(f32[704,512]{1,0:T(8,128)S(1)} %get-tuple-element.140, s32[]{:T(128)S(6)} %select_n.82, bf16[512,512]{1,0:T(8,128)(2,1)S(1)} %get-tuple-element.154, bf16[512,768]{1,0:T(8,128)(2,1)S(1)} %get-tuple-element.153, bf16[704,768]{1,0:T(8,128)(2,1)} %get-tuple-element.152, ...), kind=kOutput, calls=%fused_computation.clone.1 | convolution fusion | flops 83951616 | bytes 1541632 | tf_op jit(solution)/shard_map/while/body/dot_general | solution.py:79
  51.3 1.4 %convolution_dynamic-update-slice_fusion.2 = f32[704,512]{1,0:T(8,128)S(1)} fusion(f32[704,512]{1,0:T(8,128)S(1)} %get-tuple-element.140, s32[]{:T(128)S(6)} %select_n.82, bf16[512,512]{1,0:T(8,128)(2,1)S(1)} %get-tuple-element.154, bf16[512,768]{1,0:T(8,128)(2,1)S(1)} %get-tuple-element.153, bf16[704,768]{1,0:T(8,128)(2,1)} %get-tuple-element.152, ...), kind=kOutput, calls=%fused_computation.clone.1 | convolution fusion | flops 83951616 | bytes 1541632 | tf_op jit(solution)/shard_map/while/body/dot_general | solution.py:79
  52.8 1.4 %convolution_dynamic-update-slice_fusion.2 = f32[704,512]{1,0:T(8,128)S(1)} fusion(f32[704,512]{1,0:T(8,128)S(1)} %get-tuple-element.140, s32[]{:T(128)S(6)} %select_n.82, bf16[512,512]{1,0:T(8,128)(2,1)S(1)} %get-tuple-element.154, bf16[512,768]{1,0:T(8,128)(2,1)S(1)} %get-tuple-element.153, bf16[704,768]{1,0:T(8,128)(2,1)} %get-tuple-element.152, ...), kind=kOutput, calls=%fused_computation.clone.1 | convolution fusion | flops 83951616 | bytes 1541632 | tf_op jit(solution)/shard_map/while/body/dot_general | solution.py:79
  54.2 1.4 %convolution_dynamic-update-slice_fusion.2 = f32[704,512]{1,0:T(8,128)S(1)} fusion(f32[704,512]{1,0:T(8,128)S(1)} %get-tuple-element.140, s32[]{:T(128)S(6)} %select_n.82, bf16[512,512]{1,0:T(8,128)(2,1)S(1)} %get-tuple-element.154, bf16[512,768]{1,0:T(8,128)(2,1)S(1)} %get-tuple-element.153, bf16[704,768]{1,0:T(8,128)(2,1)} %get-tuple-element.152, ...), kind=kOutput, calls=%fused_computation.clone.1 | convolution fusion | flops 83951616 | bytes 1541632 | tf_op jit(solution)/shard_map/while/body/dot_general | solution.py:79
  55.7 1.4 %convolution_dynamic-update-slice_fusion.2 = f32[704,512]{1,0:T(8,128)S(1)} fusion(f32[704,512]{1,0:T(8,128)S(1)} %get-tuple-element.140, s32[]{:T(128)S(6)} %select_n.82, bf16[512,512]{1,0:T(8,128)(2,1)S(1)} %get-tuple-element.154, bf16[512,768]{1,0:T(8,128)(2,1)S(1)} %get-tuple-element.153, bf16[704,768]{1,0:T(8,128)(2,1)} %get-tuple-element.152, ...), kind=kOutput, calls=%fused_computation.clone.1 | convolution fusion | flops 83951616 | bytes 1541632 | tf_op jit(solution)/shard_map/while/body/dot_general | solution.py:79
  57.1 1.4 %convolution_dynamic-update-slice_fusion.2 = f32[704,512]{1,0:T(8,128)S(1)} fusion(f32[704,512]{1,0:T(8,128)S(1)} %get-tuple-element.140, s32[]{:T(128)S(6)} %select_n.82, bf16[512,512]{1,0:T(8,128)(2,1)S(1)} %get-tuple-element.154, bf16[512,768]{1,0:T(8,128)(2,1)S(1)} %get-tuple-element.153, bf16[704,768]{1,0:T(8,128)(2,1)} %get-tuple-element.152, ...), kind=kOutput, calls=%fused_computation.clone.1 | convolution fusion | flops 83951616 | bytes 1541632 | tf_op jit(solution)/shard_map/while/body/dot_general | solution.py:79
  58.6 2.5 %collective-permute-start.1 = (f32[1,704,512]{2,1,0:T(8,128)S(1)}, f32[1,704,512]{2,1,0:T(8,128)S(1)}, u32[]{:S(2)}, u32[]{:S(2)}) collective-permute-start(f32[1,704,512]{2,1,0:T(8,128)S(1)} %bitcast.23), channel_id=1, source_target_pairs={{1,0},{2,1},{3,2},{4,3},{5,4},{6,5},{7,6},{8,7},{9,8},{10,9},{11,1... | collective-permute-start | bytes 4325384 | tf_op jit(solution)/shard_map/ppermute | solution.py:22
  61.1 3.0 %collective-permute-start = (f32[1,704,512]{2,1,0:T(8,128)S(1)}, f32[1,704,512]{2,1,0:T(8,128)S(1)}, u32[]{:S(2)}, u32[]{:S(2)}) collective-permute-start(f32[1,704,512]{2,1,0:T(8,128)S(1)} %bitcast.24), channel_id=1, source_target_pairs={{0,1},{1,2},{2,3},{3,4},{4,5},{5,6},{6,7},{7,8},{8,9},{9,10},{10,1... | collective-permute-start | bytes 4325384 | tf_op jit(solution)/shard_map/ppermute | solution.py:20
  64.1 0.0 copy-done
  64.2 0.2 slice_reduce_fusion.38
  64.4 0.2 slice_reduce_fusion.37
  64.5 25.7 %collective-permute-done.1 = f32[1,704,512]{2,1,0:T(8,128)S(1)} collective-permute-done((f32[1,704,512]{2,1,0:T(8,128)S(1)}, f32[1,704,512]{2,1,0:T(8,128)S(1)}, u32[]{:S(2)}, u32[]{:S(2)}) %collective-permute-start.1) | collective-permute-done | bytes 1441824 | tf_op jit(solution)/shard_map/ppermute | solution.py:22
  90.3 4.8 %collective-permute-done = f32[1,704,512]{2,1,0:T(8,128)S(1)} collective-permute-done((f32[1,704,512]{2,1,0:T(8,128)S(1)}, f32[1,704,512]{2,1,0:T(8,128)S(1)}, u32[]{:S(2)}, u32[]{:S(2)}) %collective-permute-start) | collective-permute-done | bytes 1441824 | tf_op jit(solution)/shard_map/ppermute | solution.py:20
  95.1 0.6 select_maximum_fusion
  95.7 8.4 %fusion.10 = f32[1,704,512]{2,1,0:T(8,128)} fusion(f32[3,716,512]{2,1,0:T(8,128)S(1)} %select_maximum_fusion, f32[1,704,512]{2,1,0:T(8,128)S(1)} %collective-permute-done.1, f32[704,512]{1,0:T(8,128)S(1)} %get-tuple-element.37, f32[1,704,512]{2,1,0:T(8,128)S(1)} %collective-permute-done, f32[704]{0:T(1024)S(1)} %get-tuple-element.39, ...), kind=kLoop, calls=%fused_computation.16 | loop fusion | flops 28114944 | bytes 57782208 | tf_op jit(solution)/shard_map/jit(_where)/select_n | solution.py:100
  (15 shorter events, 0.1 us)
Async XLA Ops:
  15.0 27.3 %all-to-all-start = ((bf16[32,2,8,768]{3,1,2,0:T(2,128)(2,1)}), bf16[32,2,8,768]{3,1,2,0:T(2,128)(2,1)S(1)}, u32[]{:S(2)}, u32[]{:S(2)}) async-start(bf16[32,2,8,768]{3,1,2,0:T(2,128)(2,1)} %copy.11), calls=%async_computation | async-start | bytes 1572864 | tf_op jit(solution)/shard_map/all_to_all | solution.py:63
  42.6 21.6 %copy-start = (f32[1,3,13,704]{3,0,2,1:T(1,128)S(1)}, f32[1,3,13,704]{3,0,2,1:T(1,128)}, u32[]{:S(2)}) copy-start(f32[1,3,13,704]{3,0,2,1:T(1,128)} %param.7) | copy-start | bytes 329476
  58.6 31.7 %collective-permute-start.1 = (f32[1,704,512]{2,1,0:T(8,128)S(1)}, f32[1,704,512]{2,1,0:T(8,128)S(1)}, u32[]{:S(2)}, u32[]{:S(2)}) collective-permute-start(f32[1,704,512]{2,1,0:T(8,128)S(1)} %bitcast.23), channel_id=1, source_target_pairs={{1,0},{2,1},{3,2},{4,3},{5,4},{6,5},{7,6},{8,7},{9,8},{10,9},{11,1... | collective-permute-start | bytes 4325384 | tf_op jit(solution)/shard_map/ppermute | solution.py:22
  61.1 34.0 %collective-permute-start = (f32[1,704,512]{2,1,0:T(8,128)S(1)}, f32[1,704,512]{2,1,0:T(8,128)S(1)}, u32[]{:S(2)}, u32[]{:S(2)}) collective-permute-start(f32[1,704,512]{2,1,0:T(8,128)S(1)} %bitcast.24), channel_id=1, source_target_pairs={{0,1},{1,2},{2,3},{3,4},{4,5},{5,6},{6,7},{7,8},{8,9},{9,10},{10,1... | collective-permute-start | bytes 4325384 | tf_op jit(solution)/shard_map/ppermute | solution.py:20
where the time goes:
time: 105 us; the launch traced here: 104 us
  waiting for transfers between devices  48.7 us (46%)
  matrix products  27.6 us (26%)
  starting transfers between devices  12.6 us (12%)
  other arithmetic  11.9 us (11%)
  local copies, waits for them, and re-layouts  2.61 us (2%)
    ppermute x1, waiting for transfers between devices, padded_2(): lax.ppermute(head, axis, [((i + 1) % count, i) for i in range(ends)])  25.7 us
    all_to_all x1, waiting for transfers between devices, on_device(): lax.all_to_all(whole, 'dev', split_axis=0, concat_axis=2, tiled=True)  18.1 us
    dot_general x11, matrix products, one_block(): result = jnp.dot(coef, wtable, preferred_element_type=jnp.float32)  15.5 us
    dot_general x1, matrix products, transform_images(): jnp.einsum('kn,tan->kta', table, block, preferred_element_type=jnp.float32)  12.1 us
    select_n x1, other arithmetic, on_device(): outputs = [jnp.where((degrees >= order)[:, None], total, jnp.float32(0.0))]  8.38 us
    all_to_all x1, starting transfers between devices, on_device(): lax.all_to_all(whole, 'dev', split_axis=0, concat_axis=2, tiled=True)  7.08 us
    ppermute x1, waiting for transfers between devices, padded_2(): lax.ppermute(tail, axis, [(i, (i + 1) % count) for i in range(ends)])  4.81 us
    ppermute x1, starting transfers between devices, padded_2(): lax.ppermute(tail, axis, [(i, (i + 1) % count) for i in range(ends)])  3.03 us
  transfers between devices with their start and end apart: 3, of which 3 were waited for; matrix products, arithmetic and copies ran while one was open for 2% of the time, Pallas kernels for 0%

commit v1 on v0

v1 whole, which is shorter than its diff:
```python
import functools
import math

import jax
import jax.numpy as jnp
import numpy as np
from jax import lax
from jax.experimental import pallas as pl
from jax.experimental.pallas import tpu as pltpu
from jax.sharding import PartitionSpec as P

MESH = pl.DeviceIdType.MESH
BAND = 6
PAD = 16
F32 = jnp.float32
BF16 = jnp.bfloat16


def lon_table(nlon, norders):
    phase = (np.arange(nlon)[None, :] * np.arange(norders)[:, None]) % nlon
    angle = 2.0 * math.pi * phase / nlon
    table = np.stack([np.cos(angle), -np.sin(angle)], axis=1) / math.sqrt(nlon)
    return table.reshape(2 * norders, nlon).astype(np.float32).astype(BF16)


def time_table(ntimes, devices):
    phase = (np.arange(ntimes)[:, None] * np.arange(ntimes)[None, :]) % ntimes
    angle = 2.0 * math.pi * phase / ntimes
    cosine, sine = np.cos(angle), np.sin(angle)
    upper = np.concatenate([cosine, -sine], axis=1)
    lower = np.concatenate([sine, cosine], axis=1)
    table = np.concatenate([upper, lower], axis=0) / math.sqrt(ntimes)
    table = table.reshape(2, devices, ntimes // devices, 2 * ntimes).transpose(1, 0, 2, 3)
    return table.reshape(2 * ntimes, 2 * ntimes).astype(np.float32).astype(BF16)


def split(value):
    high = value.astype(BF16)
    low = (value - high.astype(F32)).astype(BF16)
    return high, low


def kernel(n, lat, nblk,
           images, legendre, leakage, table, wtable, out,
           img, tab, leg, leak, wt, scr, send, recv, coef, comb, bands, lk, lkt,
           img_sem, in_sem, a_send, a_recv, c_send, c_recv, out_sem):
    me = lax.axis_index("dev")
    t_local, nlat, nlon = images.shape
    rows = 2 * t_local
    nchunk = nlat // lat
    ktab = table.shape[0]
    degrees = legendre.shape[1]
    blk = degrees // nblk
    win = blk + 2 * PAD
    half = wtable.shape[0]

    def load(index, src, dst):
        return pltpu.make_async_copy(src, dst, in_sem.at[index])

    def image_copy(c, t):
        part = pl.ds(c * lat, lat)
        return pltpu.make_async_copy(images.at[t, part, :], img.at[t, part, :], img_sem.at[c, t])

    loads = [
        load(0, table, tab), load(1, legendre.at[0], leg), load(2, leakage.at[0], leak),
        load(3, wtable, wt),
    ]
    loads[0].start()
    for c in range(nchunk):
        for t in range(t_local):
            image_copy(c, t).start()
    for copy in loads[1:]:
        copy.start()

    barrier = pltpu.get_barrier_semaphore()

    def greet(o, carry):
        pl.semaphore_signal(barrier, inc=1, device_id=(lax.rem(me + o, n),), device_id_type=MESH)
        return carry

    lax.fori_loop(1, n, greet, 0)
    loads[0].wait()

    def lon_chunk(c, carry):
        for t in range(t_local):
            image_copy(c, t).wait()
            block = img[t, pl.ds(pl.multiple_of(c * lat, lat), lat), :]
            part = lax.dot_general(tab[...], block, (((1,), (1,)), ((), ())), preferred_element_type=F32)
            for j in range(lat // 128):
                scr[j, pl.ds(t, ktab, stride=t_local), :] = part[:, j * 128:(j + 1) * 128]
        for j in range(lat // 128):
            send[c, :, j * 128:(j + 1) * 128] = scr[j].astype(BF16)

        @pl.when(c == 0)
        def _():
            pl.semaphore_wait(barrier, n - 1)

        mine = pl.ds(pl.multiple_of(me * rows, rows), rows)

        def post(o, inner):
            to = lax.rem(me + o, n)
            theirs = pl.ds(pl.multiple_of(to * rows, rows), rows)
            pltpu.make_async_remote_copy(
                src_ref=send.at[c, theirs, :], dst_ref=recv.at[c, mine, :],
                send_sem=a_send.at[c], recv_sem=a_recv.at[c],
                device_id=(to,), device_id_type=MESH,
            ).start()
            return inner

        lax.fori_loop(1, n, post, 0)
        recv[c, mine, :] = send[c, mine, :]
        return carry

    lax.fori_loop(0, nchunk, lon_chunk, 0)

    loads[2].wait()
    lk[...] = jnp.zeros_like(lk)
    for d in range(3):
        lk[16 * d:16 * d + 2 * BAND + 1, 0:degrees] = leak[d]
    for j in range(lk.shape[1] // 128):
        lkt[j * 128:(j + 1) * 128, :] = lk[:, j * 128:(j + 1) * 128].T
    offset = (lax.broadcasted_iota(jnp.int32, (blk, win), 1)
              - lax.broadcasted_iota(jnp.int32, (blk, win), 0) - (PAD - BAND))

    def band_block(j, carry):
        start = pl.multiple_of(j * blk, 16)
        columns = lkt[pl.ds(start, blk), :]
        degree = start + lax.broadcasted_iota(jnp.int32, (blk, 128), 0)
        columns = jnp.where(degree >= me, columns, 0.0)
        for d in range(3):
            band = jnp.zeros((blk, win), F32)
            for k in range(2 * BAND + 1):
                band = jnp.where(offset == k, columns[:, 16 * d + k:16 * d + k + 1], band)
            high, low = split(band)
            bands[j, d, 0] = high
            bands[j, d, 1] = low
        return carry

    lax.fori_loop(0, nblk, band_block, 0)
    for d in range(3):
        coef[d, 0:PAD, :] = jnp.zeros((PAD, half), BF16)
        coef[d, PAD + degrees:, :] = jnp.zeros((PAD, half), BF16)

    @pl.when(me == 0)
    def _():
        coef[0] = jnp.zeros(coef.shape[1:], BF16)

    @pl.when(me == n - 1)
    def _():
        coef[2] = jnp.zeros(coef.shape[1:], BF16)

    loads[1].wait()
    loads[3].wait()
    away = pl.ds(0, (n - 1) * rows)
    for c in range(nchunk):
        pltpu.make_async_copy(recv.at[c, away, :], recv.at[c, away, :], a_recv.at[c]).wait()

    edges = [0] + [blk * (j + 1) + PAD for j in range(nblk - 1)] + [degrees]

    def neighbour(j, side):
        span = pl.ds(PAD + edges[j], edges[j + 1] - edges[j])
        to = jnp.maximum(me - 1, 0) if side == 0 else jnp.minimum(me + 1, n - 1)
        return pltpu.make_async_remote_copy(
            src_ref=coef.at[1, span, :], dst_ref=coef.at[2 if side == 0 else 0, span, :],
            send_sem=c_send.at[side, j], recv_sem=c_recv.at[side, j],
            device_id=(to,), device_id_type=MESH,
        )

    for j in range(nblk):
        low, high = edges[j], edges[j + 1]
        total = jnp.zeros((high - low, half), F32)
        for c in range(nchunk):
            total += lax.dot_general(
                leg[low:high, c * lat:(c + 1) * lat], recv[c],
                (((1,), (1,)), ((), ())), preferred_element_type=F32)
        degree = low + lax.broadcasted_iota(jnp.int32, (high - low, half), 0)
        coef[1, PAD + low:PAD + high, :] = jnp.where(degree >= me, total, 0.0).astype(BF16)

        @pl.when(me > 0)
        def _():
            neighbour(j, 0).start()

        @pl.when(me < n - 1)
        def _():
            neighbour(j, 1).start()

    def banded(j, d):
        window = coef[d, j * blk:j * blk + win, :]
        return (jnp.dot(bands[j, d, 0], window, preferred_element_type=F32)
                + jnp.dot(bands[j, d, 1], window, preferred_element_type=F32))

    for j in range(nblk):
        comb[j * blk:(j + 1) * blk, :] = banded(j, 1)

    def out_copy(j):
        span = pl.ds(j * blk, blk)
        return pltpu.make_async_copy(comb.at[span, :], out.at[0, span, :], out_sem.at[j])

    for j in range(nblk):
        @pl.when(me < n - 1)
        def _():
            neighbour(j, 0).wait_recv()

        @pl.when(me > 0)
        def _():
            neighbour(j, 1).wait_recv()

        high, low = split(comb[j * blk:(j + 1) * blk, :] + banded(j, 0) + banded(j, 2))
        comb[j * blk:(j + 1) * blk, :] = (
            jnp.dot(high, wt[...], preferred_element_type=F32)
            + jnp.dot(low, wt[...], preferred_element_type=F32))
        out_copy(j).start()

    for c in range(nchunk):
        pltpu.make_async_copy(send.at[c, away, :], send.at[c, away, :], a_send.at[c]).wait()
    for j in range(nblk):
        @pl.when(me > 0)
        def _():
            neighbour(j, 0).wait_send()

        @pl.when(me < n - 1)
        def _():
            neighbour(j, 1).wait_send()

        out_copy(j).wait()


def on_device(n, images, legendre, leakage):
    t_local, nlat, nlon = images.shape
    degrees = legendre.shape[1]
    ntimes = t_local * n
    half = 2 * ntimes
    lat = 256 if nlat % 256 == 0 else 128
    nchunk = nlat // lat
    nblk = 4 if half <= 1024 else degrees // 64
    blk = degrees // nblk
    table = jnp.asarray(lon_table(nlon, n))
    wtable = jnp.asarray(time_table(ntimes, n))
    wide = -(-degrees // 128) * 128
    anywhere = pl.BlockSpec(memory_space=pl.ANY)
    return pl.pallas_call(
        functools.partial(kernel, n, lat, nblk),
        out_shape=jax.ShapeDtypeStruct((1, degrees, half), F32),
        in_specs=[anywhere] * 5,
        out_specs=anywhere,
        scratch_shapes=[
            pltpu.VMEM(images.shape, BF16),
            pltpu.VMEM(table.shape, BF16),
            pltpu.VMEM(legendre.shape[1:], BF16),
            pltpu.VMEM(leakage.shape[1:], F32),
            pltpu.VMEM(wtable.shape, BF16),
            pltpu.VMEM((lat // 128, 2 * n * t_local, 128), F32),
            pltpu.VMEM((nchunk, half, lat), BF16),
            pltpu.VMEM((nchunk, half, lat), BF16),
            pltpu.VMEM((3, degrees + 2 * PAD, half), BF16),
            pltpu.VMEM((degrees, half), F32),
            pltpu.VMEM((nblk, 3, 2, blk, blk + 2 * PAD), BF16),
            pltpu.VMEM((128, wide), F32),
            pltpu.VMEM((wide, 128), F32),
            pltpu.SemaphoreType.DMA((nchunk, t_local)),
            pltpu.SemaphoreType.DMA((4,)),
            pltpu.SemaphoreType.DMA((nchunk,)),
            pltpu.SemaphoreType.DMA((nchunk,)),
            pltpu.SemaphoreType.DMA((2, nblk)),
            pltpu.SemaphoreType.DMA((2, nblk)),
            pltpu.SemaphoreType.DMA((nblk,)),
        ],
        compiler_params=pltpu.CompilerParams(
            collective_id=0, has_side_effects=True, vmem_limit_bytes=66_000_000),
    )(images, legendre, leakage, table, wtable)


def solution(mesh):
    placed = (P("dev", None, None), P("dev", None, None), P("dev", None, None, None))
    return jax.shard_map(
        functools.partial(on_device, mesh.shape["dev"]),
        mesh=mesh, in_specs=placed, out_specs=P("dev", None, None), check_vma=False,
    )
```

time: 105 us -> 54.8 us (0.52)
  Pallas kernels: 0 us -> 50.5 us
  waiting for transfers between devices: 48.7 us -> 0 us
  matrix products: 27.6 us -> 0 us
  starting transfers between devices: 12.6 us -> 0 us
  other arithmetic: 11.9 us -> 0 us
  local copies, waits for them, and re-layouts: 2.61 us -> 4.14 us
    pallas_call x0 -> x1, Pallas kernels: none -> 50.5 us  [on_device(): pl.pallas_call(functools.partial(kernel, n, lat, nblk), out_shape=jax.Sha...]
    ppermute x2 -> x0, waiting for transfers between devices: 30.6 us -> none  [the longest x1 25.7 us: padded_2(): lax.ppermute(head, axis, [((i + 1) % count, i) for i in range(ends)])]
    dot_general x12 -> x0, matrix products: 27.6 us -> none  [the longest x11 15.5 us: one_block(): result = jnp.dot(coef, wtable, preferred_element_type=jnp.float32)]
    all_to_all x1 -> x0, waiting for transfers between devices: 18.1 us -> none  [on_device(): lax.all_to_all(whole, 'dev', split_axis=0, concat_axis=2, tiled=True)]
    select_n x1 -> x0, other arithmetic: 8.38 us -> none  [on_device(): outputs = [jnp.where((degrees >= order)[:, None], total, jnp.float32(0.0))]]
    all_to_all x1 -> x0, starting transfers between devices: 7.08 us -> none  [on_device(): lax.all_to_all(whole, 'dev', split_axis=0, concat_axis=2, tiled=True)]
    ppermute x2 -> x0, starting transfers between devices: 5.56 us -> none  [the longest x1 3.03 us: padded_2(): lax.ppermute(tail, axis, [(i, (i + 1) % count) for i in range(ends)])]
    unnamed x3 -> x2, local copies, waits for them, and re-layouts: 0.02 us -> 4.14 us
  transfers between devices with their start and end apart: 3 -> 0, of which waited for: 3 -> 0; matrix products, arithmetic and copies ran while one was open for 2% -> 0% of each run, Pallas kernels for 0% -> 0%
where the time goes in v1:
time: 54.8 us; the launch traced here: 54.7 us
  Pallas kernels  50.5 us (92%)
  local copies, waits for them, and re-layouts  4.14 us (8%)
    pallas_call x1, Pallas kernels, on_device(): pl.pallas_call(functools.partial(kernel, n, lat, nblk), out_shape=jax.Sha...  50.5 us
    unnamed x2, local copies, waits for them, and re-layouts  4.14 us

profile of v1, /device:TPU:1, one launch (start us, length us, event | category | flops | bytes accessed | tf_op | source)
XLA Modules:
  0.0 54.7 jit_solution(3500518184306837931)
XLA Ops:
  0.0 1.6 %copy.6.leakage = f32[1,3,13,704]{3,2,1,0:T(8,128)} copy(f32[1,3,13,704]{3,0,2,1:T(1,128)} %param.7) | data formatting | bytes 219648 | tf_op args[2]
  1.6 50.5 %shard_map.55 = f32[1,704,512]{2,1,0:T(8,128)} custom-call(bf16[8,768,1536]{2,1,0:T(8,128)(2,1)} %images.1, bf16[1,704,768]{2,1,0:T(8,128)(2,1)} %legendre.1, f32[1,3,13,704]{3,2,1,0:T(8,128)} %copy.6.leakage, bf16[64,1536]{1,0:T(8,128)(2,1)} %constant.4.clone.table, bf16[512,512]{1,0:T(8,128)(2,1)} %constant.5.clone.wtable), custom_call_target="tpu_custom_call" | custom-call | tf_op jit(solution)/shard_map/pallas_call | solution.py:241
  52.1 2.6 %copy.8 = f32[1,704,512]{2,1,0:T(8,128)} copy(f32[1,704,512]{2,1,0:T(8,128)} %shard_map.55) | data formatting | bytes 2883584

commit v2 on v1

v2 whole, which is shorter than its diff:
```python
import functools
import math

import jax
import jax.numpy as jnp
import numpy as np
from jax import lax
from jax.experimental import pallas as pl
from jax.experimental.pallas import tpu as pltpu
from jax.sharding import PartitionSpec as P

MESH = pl.DeviceIdType.MESH
BAND = 6
PAD = 16
F32 = jnp.float32
BF16 = jnp.bfloat16


def lon_table(nlon, norders):
    phase = (np.arange(nlon)[None, :] * np.arange(norders)[:, None]) % nlon
    angle = 2.0 * math.pi * phase / nlon
    table = np.stack([np.cos(angle), -np.sin(angle)], axis=1) / math.sqrt(nlon)
    return table.reshape(2 * norders, nlon).astype(np.float32).astype(BF16)


def time_table(ntimes, devices):
    phase = (np.arange(ntimes)[:, None] * np.arange(ntimes)[None, :]) % ntimes
    angle = 2.0 * math.pi * phase / ntimes
    cosine, sine = np.cos(angle), np.sin(angle)
    upper = np.concatenate([cosine, -sine], axis=1)
    lower = np.concatenate([sine, cosine], axis=1)
    table = np.concatenate([upper, lower], axis=0) / math.sqrt(ntimes)
    table = table.reshape(2, devices, ntimes // devices, 2 * ntimes).transpose(1, 0, 2, 3)
    return table.reshape(2 * ntimes, 2 * ntimes).astype(np.float32).astype(BF16)


def split(value):
    high = value.astype(BF16)
    low = (value - high.astype(F32)).astype(BF16)
    return high, low


def kernel(n, lat, nblk, ngrp,
           images, legendre, leakage, table, wtable, out,
           img, tab, leg, leak, wt, scr, send, recv, coef, acc, bands, lk, lkt,
           img_sem, in_sem, a_send, a_recv, c_send, c_recv, out_sem):
    me = lax.axis_index("dev")
    t_local, nlat, nlon = images.shape
    rows = 2 * t_local
    nchunk = nlat // lat
    ktab = 2 * n
    grp = n // ngrp
    wide = grp * rows
    group, place = me // grp, lax.rem(me, grp)
    degrees = legendre.shape[1]
    blk = degrees // nblk
    win = blk + 2 * PAD
    half = wtable.shape[0]

    def load(index, src, dst):
        return pltpu.make_async_copy(src, dst, in_sem.at[index])

    def image_copy(c, t):
        part = pl.ds(c * lat, lat)
        return pltpu.make_async_copy(images.at[t, part, :], img.at[t, part, :], img_sem.at[c, t])

    loads = [
        load(0, table, tab), load(1, legendre.at[0], leg), load(2, leakage, leak),
        load(3, wtable, wt),
    ]
    loads[0].start()
    for c in range(nchunk):
        for t in range(t_local):
            image_copy(c, t).start()
    for copy in loads[1:]:
        copy.start()

    barrier = pltpu.get_barrier_semaphore()

    def greet(o, carry):
        pl.semaphore_signal(barrier, inc=1, device_id=(lax.rem(me + o, n),), device_id_type=MESH)
        return carry

    lax.fori_loop(1, n, greet, 0)
    loads[0].wait()

    def lon_chunk(c, carry):
        for t in range(t_local):
            image_copy(c, t).wait()
        block = img[:, pl.ds(pl.multiple_of(c * lat, lat), lat), :].reshape(t_local * lat, nlon)
        whole = jnp.dot(block, tab[...], preferred_element_type=F32)
        for t in range(t_local):
            part = whole[t * lat:(t + 1) * lat].T[:ktab]
            for j in range(lat // 128):
                scr[j, pl.ds(t, ktab, stride=t_local), :] = part[:, j * 128:(j + 1) * 128]
        for j in range(lat // 128):
            send[c, :, j * 128:(j + 1) * 128] = scr[j].astype(BF16)

        @pl.when(c == 0)
        def _():
            pl.semaphore_wait(barrier, n - 1)

        mine = pl.ds(pl.multiple_of(me * rows, rows), rows)

        def post(o, inner):
            step, seat = o // grp, lax.rem(o, grp)
            to = lax.rem(group + step, ngrp) * grp + lax.rem(place + seat, grp)
            theirs = pl.ds(pl.multiple_of(to * rows, rows), rows)
            pltpu.make_async_remote_copy(
                src_ref=send.at[c, theirs, :], dst_ref=recv.at[c, mine, :],
                send_sem=a_send.at[c], recv_sem=a_recv.at[step, c],
                device_id=(to,), device_id_type=MESH,
            ).start()
            return inner

        lax.fori_loop(1, n, post, 0)
        recv[c, mine, :] = send[c, mine, :]
        return carry

    lax.fori_loop(0, nchunk, lon_chunk, 0)

    loads[2].wait()
    lk[...] = jnp.zeros_like(lk)
    for d in range(3):
        for k in range(2 * BAND + 1):
            lk[16 * d + k:16 * d + k + 1, 0:degrees] = leak[k, d]
    for j in range(lk.shape[1] // 128):
        lkt[j * 128:(j + 1) * 128, :] = lk[:, j * 128:(j + 1) * 128].T
    offset = (lax.broadcasted_iota(jnp.int32, (blk, win), 1)
              - lax.broadcasted_iota(jnp.int32, (blk, win), 0) - (PAD - BAND))

    def band_block(j, carry):
        start = pl.multiple_of(j * blk, 16)
        columns = lkt[pl.ds(start, blk), :]
        degree = start + lax.broadcasted_iota(jnp.int32, (blk, 128), 0)
        columns = jnp.where(degree >= me, columns, 0.0)
        for d in range(3):
            band = jnp.zeros((blk, win), F32)
            for k in range(2 * BAND + 1):
                band = jnp.where(offset == k, columns[:, 16 * d + k:16 * d + k + 1], band)
            high, low = split(band)
            bands[j, d, 0:blk, :] = high
            bands[j, d, blk:, :] = low
        return carry

    lax.fori_loop(0, nblk, band_block, 0)
    margin = jnp.zeros((PAD, wide), BF16)
    for d in range(3):
        for g in range(ngrp):
            coef[d, g, 0:PAD, :] = margin
            coef[d, g, PAD + degrees:, :] = margin
    acc[...] = jnp.zeros_like(acc)
    loads[1].wait()
    loads[3].wait()

    def accumulate(d, g):
        rows_of = pl.ds(pl.multiple_of(g * wide, wide), wide)
        for j in range(nblk):
            span = slice(j * blk, (j + 1) * blk)
            both = jnp.dot(bands[j, d], coef[d, g, j * blk:j * blk + win, :], preferred_element_type=F32)
            high, low = split(both[:blk] + both[blk:])
            acc[span, :] += (jnp.dot(high, wt[rows_of, :], preferred_element_type=F32)
                             + jnp.dot(low, wt[rows_of, :], preferred_element_type=F32))

    def neighbour(i, g, side):
        span = pl.ds(PAD, degrees)
        to = jnp.maximum(me - 1, 0) if side == 0 else jnp.minimum(me + 1, n - 1)
        return pltpu.make_async_remote_copy(
            src_ref=coef.at[1, g, span, :], dst_ref=coef.at[2 if side == 0 else 0, g, span, :],
            send_sem=c_send.at[side, i], recv_sem=c_recv.at[side, i],
            device_id=(to,), device_id_type=MESH,
        )

    def nth(i, device):
        return lax.rem(device // grp - i + ngrp, ngrp)

    def coef_group(i, carry):
        for c in range(nchunk):
            @pl.when(i == 0)
            def _():
                piece = recv.at[c, pl.ds(0, (grp - 1) * rows), :]
                pltpu.make_async_copy(piece, piece, a_recv.at[0, c]).wait()

            @pl.when(i > 0)
            def _():
                piece = recv.at[c, pl.ds(0, wide), :]
                pltpu.make_async_copy(piece, piece, a_recv.at[i, c]).wait()

        g = nth(i, me)
        rows_of = pl.ds(pl.multiple_of(g * wide, wide), wide)
        total = jnp.zeros((degrees, wide), F32)
        for c in range(nchunk):
            total += lax.dot_general(
                leg[:, c * lat:(c + 1) * lat], recv[c, rows_of, :],
                (((1,), (1,)), ((), ())), preferred_element_type=F32)
        degree = lax.broadcasted_iota(jnp.int32, (degrees, wide), 0)
        coef[1, g, PAD:PAD + degrees, :] = jnp.where(degree >= me, total, 0.0).astype(BF16)

        @pl.when(me > 0)
        def _():
            neighbour(i, g, 0).start()

        @pl.when(me < n - 1)
        def _():
            neighbour(i, g, 1).start()

        accumulate(1, g)
        return carry

    lax.fori_loop(0, ngrp, coef_group, 0)

    def side_group(i, carry):
        @pl.when(me < n - 1)
        def _():
            g = nth(i, me + 1)
            neighbour(i, g, 0).wait_recv()
            accumulate(2, g)

        @pl.when(me > 0)
        def _():
            g = nth(i, me - 1)
            neighbour(i, g, 1).wait_recv()
            accumulate(0, g)

        return carry

    lax.fori_loop(0, ngrp, side_group, 0)
    result = pltpu.make_async_copy(acc, out.at[0], out_sem)
    result.start()

    away = pl.ds(0, (n - 1) * rows)
    for c in range(nchunk):
        pltpu.make_async_copy(send.at[c, away, :], send.at[c, away, :], a_send.at[c]).wait()

    def sent(i, carry):
        g = nth(i, me)

        @pl.when(me > 0)
        def _():
            neighbour(i, g, 0).wait_send()

        @pl.when(me < n - 1)
        def _():
            neighbour(i, g, 1).wait_send()

        return carry

    lax.fori_loop(0, ngrp, sent, 0)
    result.wait()


def on_device(n, images, legendre, leakage):
    t_local, nlat, nlon = images.shape
    degrees = legendre.shape[1]
    ntimes = t_local * n
    half = 2 * ntimes
    lat = 256 if nlat % 256 == 0 else 128
    nchunk = nlat // lat
    nblk = 4 if half <= 1024 else degrees // 64
    blk = degrees // nblk
    ngrp = half // 128
    table = lon_table(nlon, n).T
    table = jnp.asarray(np.concatenate([table, np.zeros((nlon, -2 * n % 128), BF16)], axis=1))
    leakage = leakage.transpose(2, 1, 0, 3)
    wtable = jnp.asarray(time_table(ntimes, n))
    wide = -(-degrees // 128) * 128
    anywhere = pl.BlockSpec(memory_space=pl.ANY)
    return pl.pallas_call(
        functools.partial(kernel, n, lat, nblk, ngrp),
        out_shape=jax.ShapeDtypeStruct((1, degrees, half), F32),
        in_specs=[anywhere] * 5,
        out_specs=anywhere,
        scratch_shapes=[
            pltpu.VMEM(images.shape, BF16),
            pltpu.VMEM(table.shape, BF16),
            pltpu.VMEM(legendre.shape[1:], BF16),
            pltpu.VMEM(leakage.shape, F32),
            pltpu.VMEM(wtable.shape, BF16),
            pltpu.VMEM((lat // 128, 2 * n * t_local, 128), F32),
            pltpu.VMEM((nchunk, half, lat), BF16),
            pltpu.VMEM((nchunk, half, lat), BF16),
            pltpu.VMEM((3, ngrp, degrees + 2 * PAD, half // ngrp), BF16),
            pltpu.VMEM((degrees, half), F32),
            pltpu.VMEM((nblk, 3, 2 * blk, blk + 2 * PAD), BF16),
            pltpu.VMEM((128, wide), F32),
            pltpu.VMEM((wide, 128), F32),
            pltpu.SemaphoreType.DMA((nchunk, t_local)),
            pltpu.SemaphoreType.DMA((4,)),
            pltpu.SemaphoreType.DMA((nchunk,)),
            pltpu.SemaphoreType.DMA((ngrp, nchunk)),
            pltpu.SemaphoreType.DMA((2, ngrp)),
            pltpu.SemaphoreType.DMA((2, ngrp)),
            pltpu.SemaphoreType.DMA,
        ],
        compiler_params=pltpu.CompilerParams(
            collective_id=0, has_side_effects=True, vmem_limit_bytes=66_000_000),
    )(images, legendre, leakage, table, wtable)


def solution(mesh):
    placed = (P("dev", None, None), P("dev", None, None), P("dev", None, None, None))
    return jax.shard_map(
        functools.partial(on_device, mesh.shape["dev"]),
        mesh=mesh, in_specs=placed, out_specs=P("dev", None, None), check_vma=False,
    )
```

time: 54.8 us -> 48.7 us (0.89)
  the two profiles are of different devices: /device:TPU:1 before, /device:TPU:21 now
where the time goes in v2:
time: 48.7 us; the launch traced here: 48.6 us
  Pallas kernels  44.4 us (91%)
  local copies, waits for them, and re-layouts  4.14 us (9%)
    pallas_call x1, Pallas kernels, on_device(): pl.pallas_call(functools.partial(kernel, n, lat, nblk, ngrp), out_shape=j...  44.4 us
    unnamed x2, local copies, waits for them, and re-layouts  4.14 us

profile of v2, /device:TPU:21, one launch (start us, length us, event | category | flops | bytes accessed | tf_op | source)
XLA Modules:
  0.0 48.6 jit_solution(14570824578886540891)
XLA Ops:
  0.0 1.6 %copy.8 = f32[1,3,13,704]{3,0,1,2:T(1,128)} copy(f32[1,3,13,704]{3,0,2,1:T(1,128)} %param.7) | data formatting | bytes 219648 | tf_op args[2]
  1.6 44.4 %shard_map.55 = f32[1,704,512]{2,1,0:T(8,128)} custom-call(bf16[8,768,1536]{2,1,0:T(8,128)(2,1)} %images.1, bf16[1,704,768]{2,1,0:T(8,128)(2,1)} %legendre.1, f32[13,3,1,704]{3,2,1,0:T(1,128)} %bitcast.3, bf16[1536,128]{1,0:T(8,128)(2,1)} %constant.4.clone.table, bf16[512,512]{1,0:T(8,128)(2,1)} %constant.5.clone.wtable), custom_call_target="tpu_custom_call" | custom-call | tf_op jit(solution)/shard_map/pallas_call | solution.py:268
  46.0 2.6 %copy.10 = f32[1,704,512]{2,1,0:T(8,128)} copy(f32[1,704,512]{2,1,0:T(8,128)} %shard_map.55) | data formatting | bytes 2883584

commit v3 on v2

--- a/solution.py
+++ b/solution.py
@@ -123,7 +123,7 @@
     lk[...] = jnp.zeros_like(lk)
     for d in range(3):
         for k in range(2 * BAND + 1):
-            lk[16 * d + k:16 * d + k + 1, 0:degrees] = leak[k, d]
+            lk[16 * d + k:16 * d + k + 1, 0:degrees] = leak[d, k]
     for j in range(lk.shape[1] // 128):
         lkt[j * 128:(j + 1) * 128, :] = lk[:, j * 128:(j + 1) * 128].T
     offset = (lax.broadcasted_iota(jnp.int32, (blk, win), 1)
@@ -149,18 +149,19 @@
         for g in range(ngrp):
             coef[d, g, 0:PAD, :] = margin
             coef[d, g, PAD + degrees:, :] = margin
-    acc[...] = jnp.zeros_like(acc)
     loads[1].wait()
     loads[3].wait()
 
     def accumulate(d, g):
-        rows_of = pl.ds(pl.multiple_of(g * wide, wide), wide)
+        columns_of = pl.ds(pl.multiple_of(g * wide, wide), wide)
         for j in range(nblk):
             span = slice(j * blk, (j + 1) * blk)
             both = jnp.dot(bands[j, d], coef[d, g, j * blk:j * blk + win, :], preferred_element_type=F32)
-            high, low = split(both[:blk] + both[blk:])
-            acc[span, :] += (jnp.dot(high, wt[rows_of, :], preferred_element_type=F32)
-                             + jnp.dot(low, wt[rows_of, :], preferred_element_type=F32))
+            both = both[:blk] + both[blk:]
+            if d == 1:
+                acc[span, columns_of] = both
+            else:
+                acc[span, columns_of] += both
 
     def neighbour(i, g, side):
         span = pl.ds(PAD, degrees)
@@ -225,8 +226,21 @@
         return carry
 
     lax.fori_loop(0, ngrp, side_group, 0)
-    result = pltpu.make_async_copy(acc, out.at[0], out_sem)
-    result.start()
+
+    def out_copy(j):
+        span = pl.ds(j * blk, blk)
+        return pltpu.make_async_copy(acc.at[span, :], out.at[0, span, :], out_sem.at[j])
+
+    depth = min(half, 512)
+    for j in range(nblk):
+        span = slice(j * blk, (j + 1) * blk)
+        high, low = split(acc[span, :])
+        total = jnp.zeros((blk, half), F32)
+        for k in range(0, half, depth):
+            total += (jnp.dot(high[:, k:k + depth], wt[k:k + depth, :], preferred_element_type=F32)
+                      + jnp.dot(low[:, k:k + depth], wt[k:k + depth, :], preferred_element_type=F32))
+        acc[span, :] = total
+        out_copy(j).start()
 
     away = pl.ds(0, (n - 1) * rows)
     for c in range(nchunk):
@@ -246,7 +260,8 @@
         return carry
 
     lax.fori_loop(0, ngrp, sent, 0)
-    result.wait()
+    for j in range(nblk):
+        out_copy(j).wait()
 
 
 def on_device(n, images, legendre, leakage):
@@ -261,7 +276,7 @@
     ngrp = half // 128
     table = lon_table(nlon, n).T
     table = jnp.asarray(np.concatenate([table, np.zeros((nlon, -2 * n % 128), BF16)], axis=1))
-    leakage = leakage.transpose(2, 1, 0, 3)
+    leakage = leakage.transpose(1, 2, 0, 3)
     wtable = jnp.asarray(time_table(ntimes, n))
     wide = -(-degrees // 128) * 128
     anywhere = pl.BlockSpec(memory_space=pl.ANY)
@@ -290,7 +305,7 @@
             pltpu.SemaphoreType.DMA((ngrp, nchunk)),
             pltpu.SemaphoreType.DMA((2, ngrp)),
             pltpu.SemaphoreType.DMA((2, ngrp)),
-            pltpu.SemaphoreType.DMA,
+            pltpu.SemaphoreType.DMA((nblk,)),
         ],
         compiler_params=pltpu.CompilerParams(
             collective_id=0, has_side_effects=True, vmem_limit_bytes=66_000_000),

time: 48.7 us -> 46.1 us (0.947)
  the two profiles are of different devices: /device:TPU:21 before, /device:TPU:19 now
where the time goes in v3:
time: 46.1 us; the launch traced here: 45.9 us
  Pallas kernels  43.4 us (94%)
  local copies, waits for them, and re-layouts  2.57 us (6%)
    pallas_call x1, Pallas kernels, on_device(): pl.pallas_call(functools.partial(kernel, n, lat, nblk, ngrp), out_shape=j...  43.4 us
    unnamed x1, local copies, waits for them, and re-layouts  2.57 us

profile of v3, /device:TPU:19, one launch (start us, length us, event | category | flops | bytes accessed | tf_op | source)
XLA Modules:
  0.0 45.9 jit_solution(4645587018504664277)
XLA Ops:
  0.0 43.4 %shard_map.55 = f32[1,704,512]{2,1,0:T(8,128)} custom-call(bf16[8,768,1536]{2,1,0:T(8,128)(2,1)} %images.1, bf16[1,704,768]{2,1,0:T(8,128)(2,1)} %legendre.1, f32[3,13,1,704]{3,2,1,0:T(1,128)} %bitcast.1, bf16[1536,128]{1,0:T(8,128)(2,1)} %constant.4.clone.table, bf16[512,512]{1,0:T(8,128)(2,1)} %constant.5.clone.wtable), custom_call_target="tpu_custom_call" | custom-call | tf_op jit(solution)/shard_map/pallas_call | solution.py:283
  43.4 2.6 %copy.7 = f32[1,704,512]{2,1,0:T(8,128)} copy(f32[1,704,512]{2,1,0:T(8,128)} %shard_map.55) | data formatting | bytes 2883584
